TPU v7x, 32 devices: a whole 2x2x4 slice. The times are simulated.
32 devices in a mesh: grp: 1, date: 4 (over y, x), shard: 8 (over z, core).
Axes of the slice: x: 2, y: 2, z: 4, core: 2. Of those that a mesh axis runs over, the one named last changes fastest.
Arguments:
- echo_spectra: bfloat16 [4, 2, 128, 8192], P(('grp', 'date'), None, 'shard'), may hold values from -6 to 6
- range_reference: float32 [2, 8192], replicated, may hold values from -5 to 5
- azimuth_reference: bfloat16 [2, 128, 8192], P(None, None, 'shard'), may hold values from -5 to 5
- block_owner: int32 [4, 64], P(('grp', 'date')), may hold values from 0 to 7, as said below
- block_slot: int32 [4, 64], P(('grp', 'date')), may hold values from 0 to 15, as said below
- kernel_index: int32 [4, 64], P(('grp', 'date')), may hold values from 0 to 7
Outputs:
- filtered: bfloat16 [4, 128, 2, 2, 128, 128], P(('grp', 'date'), 'shard')
Inputs may be any that keep to these rules, and one draw needn't show every extreme that they name: `block_owner`: every date carries the same owners (the stack is coregistered onto one map grid). Within a date, the 8 blocks of one range-column group name any one owner at most 2 times, and some group names some owner exactly 2 times; every owner is named by at most 16 blocks, and some owner by exactly 16. `block_slot`: every date carries the same slots. Within a date, blocks that name the same owner have distinct slots.
All inputs are finite; a program needn't handle non-finite values.
Results may differ from a plain program's by a relative error of at most 0.017.
Values may be sent and summed in bfloat16 or wider, within the bound.
A program may use at most 128 MiB of HBM per device.

v0:
```python
import math
import jax
import jax.numpy as jnp
from jax import lax
from jax.sharding import PartitionSpec as P

RNG = 8192
RSPLIT = 64
BLK = 128
NSUB = 8
BLK_DEV = 8


def passed_along(value, axis, steps):
    count = lax.axis_size(axis)
    pairs = [(source, (source + steps) % count) for source in range(count)]
    return lax.ppermute(value, axis, pairs)


def dft_block(size, sign):
    index = jnp.arange(size, dtype=jnp.int32)
    phase = index[:, None] * index[None, :] % size
    angle = 2.0 * math.pi / size * phase.astype(jnp.float32)
    scale = 1.0 / math.sqrt(size)
    cosine = jnp.cos(angle) * scale
    sine = sign * jnp.sin(angle) * scale
    table = jnp.stack([jnp.stack([cosine, -sine]), jnp.stack([sine, cosine])])
    return jnp.transpose(table, (0, 2, 1, 3)).astype(jnp.bfloat16)


def twiddle(first_len, second_len, total):
    left = jnp.arange(first_len, dtype=jnp.int32)
    right = jnp.arange(second_len, dtype=jnp.int32)
    phase = left[:, None] * right[None, :] % total
    angle = 2.0 * math.pi / total * phase.astype(jnp.float32)
    return (jnp.cos(angle), jnp.sin(angle))


def kernel_table():
    offset = (jnp.arange(NSUB, dtype=jnp.float32) + 0.5) / NSUB
    cells = jnp.arange(BLK, dtype=jnp.float32)
    dist = cells[None, None, :] - cells[None, :, None] - offset[:, None, None]
    window = jnp.where(jnp.abs(dist) < 4.0, 0.5 + 0.5 * jnp.cos(math.pi * dist / 4.0), 0.0)
    return (jnp.sinc(dist) * window).astype(jnp.bfloat16)


def bdot(form, left, right):
    return jnp.einsum(form, left, right, preferred_element_type=jnp.float32)


def range_compress(spectra, reference):
    real_in = spectra[0].astype(jnp.float32)
    imag_in = spectra[1].astype(jnp.float32)
    matched = jnp.stack(
        [
            real_in * reference[0] + imag_in * reference[1],
            imag_in * reference[0] - real_in * reference[1],
        ]
    ).astype(jnp.bfloat16)
    count = spectra.shape[1]
    outer_len = RSPLIT
    inner_len = RNG // RSPLIT
    shaped = matched.reshape(2, count, outer_len, inner_len)
    section = bdot("cnek,epkb->cpnb", dft_block(outer_len, 1), shaped)
    twc, tws = twiddle(outer_len, inner_len, RNG)
    first = jnp.stack(
        [section[0] * twc - section[1] * tws, section[0] * tws + section[1] * twc]
    ).astype(jnp.bfloat16)
    second = bdot("cmek,epnk->cpmn", dft_block(inner_len, 1), first)
    return second.reshape(2, count, RNG).astype(jnp.bfloat16)


def azimuth_focus(columns, reference):
    count = columns.shape[1]
    doppler = bdot("cuep,epk->cuk", dft_block(count, -1), columns)
    ref_re = reference[0].astype(jnp.float32)
    ref_im = reference[1].astype(jnp.float32)
    shaped = jnp.stack(
        [doppler[0] * ref_re - doppler[1] * ref_im, doppler[0] * ref_im + doppler[1] * ref_re]
    ).astype(jnp.bfloat16)
    return bdot("cuep,epk->cuk", dft_block(count, 1), shaped).astype(jnp.bfloat16)


def resample(blocks, kinds):
    count = blocks.shape[0]
    picker = (kinds[:, None] == jnp.arange(NSUB, dtype=jnp.int32)[None, :]).astype(jnp.bfloat16)
    table = kernel_table().reshape(NSUB, BLK * BLK)
    kernels = (
        jnp.dot(picker, table, preferred_element_type=jnp.float32)
        .astype(jnp.bfloat16)
        .reshape(count, BLK, BLK)
    )
    return bdot("nij,ncjk->ncik", kernels, blocks).astype(jnp.bfloat16)


def cross(first, second):
    fre = first[:, 0].astype(jnp.float32)
    fim = first[:, 1].astype(jnp.float32)
    sre = second[:, 0].astype(jnp.float32)
    sim = second[:, 1].astype(jnp.float32)
    return jnp.stack([fre * sre + fim * sim, fim * sre - fre * sim], axis=1)


def goldstein(patches):
    forward = dft_block(BLK, -1)
    backward = dft_block(BLK, 1)
    rows = bdot("cuei,npeij->npcuj", forward, patches).astype(jnp.bfloat16)
    spectrum = bdot("npeuj,cvej->npcuv", rows, forward)
    power = spectrum[:, :, 0] ** 2 + spectrum[:, :, 1] ** 2
    smooth = jnp.zeros_like(power)
    for down in (-1, 0, 1):
        for across in (-1, 0, 1):
            smooth = smooth + jnp.roll(power, (down, across), axis=(-2, -1))
    smooth = smooth / 9.0
    level = jnp.mean(smooth, axis=(-2, -1), keepdims=True)
    weight = jnp.sqrt(jnp.sqrt(smooth / (level + 1e-06)))
    weighted = (spectrum * weight[:, :, None]).astype(jnp.bfloat16)
    back = bdot("cuei,npeij->npcuj", backward, weighted).astype(jnp.bfloat16)
    return bdot("npeuj,cvej->npcuv", back, backward).astype(jnp.bfloat16)


def body(echo_spectra, range_reference, azimuth_reference, block_owner, block_slot, kernel_index):
    shards = lax.axis_size("shard")
    most = max(2, 2 * BLK_DEV // shards)
    capacity = min(2 * BLK_DEV, shards * most)
    outgoing = shards * most
    compressed = range_compress(echo_spectra[0], range_reference)
    columns = lax.all_to_all(compressed, "shard", split_axis=2, concat_axis=1, tiled=True)
    image = azimuth_focus(columns, azimuth_reference)
    row_blocks = image.shape[1] // BLK
    col_blocks = image.shape[2] // BLK
    blocks = image.reshape(2, row_blocks, BLK, col_blocks, BLK)
    blocks = jnp.transpose(blocks, (1, 3, 0, 2, 4)).reshape(BLK_DEV, 2, BLK, BLK)
    owners = block_owner[0]
    slots = block_slot[0]
    kinds = kernel_index[0]
    total = owners.shape[0]
    me_index = lax.axis_index("shard")
    numbers = jnp.arange(total, dtype=jnp.int32)
    sender = numbers // BLK_DEV
    earlier = (
        (sender[:, None] == sender[None, :])
        & (owners[:, None] == owners[None, :])
        & (numbers[None, :] < numbers[:, None])
    )
    rank = jnp.sum(earlier.astype(jnp.int32), axis=1)
    target = owners * most + rank
    my_target = lax.dynamic_slice_in_dim(target, me_index * BLK_DEV, BLK_DEV)
    chooser = (my_target[None, :] == jnp.arange(outgoing, dtype=jnp.int32)[:, None]).astype(
        jnp.bfloat16
    )
    outbox = bdot("en,nxyz->exyz", chooser, blocks).astype(jnp.bfloat16)
    outbox = outbox.reshape(shards, most, 2, BLK, BLK)
    inbox = lax.all_to_all(outbox, "shard", split_axis=0, concat_axis=0, tiled=True).reshape(
        outgoing, 2, BLK, BLK
    )
    entry = sender * most + rank
    hits = owners == me_index
    slot_hit = (slots[None, :] == jnp.arange(capacity, dtype=jnp.int32)[:, None]) & hits[None, :]
    entry_hit = entry[:, None] == jnp.arange(outgoing, dtype=jnp.int32)[None, :]
    placing = jnp.dot(slot_hit.astype(jnp.float32), entry_hit.astype(jnp.float32)).astype(
        jnp.bfloat16
    )
    tile = bdot("qe,exyz->qxyz", placing, inbox).astype(jnp.bfloat16)
    slot_kinds = jnp.sum(slot_hit.astype(jnp.int32) * kinds[None, :], axis=1)
    tile = resample(tile, slot_kinds)
    following = passed_along(tile, "date", -1)
    second = passed_along(tile, "date", -2)
    pairs = jnp.stack([cross(tile, following), cross(tile, second)], axis=1).astype(jnp.bfloat16)
    return goldstein(pairs)[None]


def solution(mesh):
    in_specs = (
        P(("grp", "date"), None, "shard", None),
        P(),
        P(None, None, "shard"),
        P(("grp", "date"), None),
        P(("grp", "date"), None),
        P(("grp", "date"), None),
    )
    out_specs = P(("grp", "date"), "shard", None, None, None, None)
    return jax.shard_map(body, mesh=mesh, in_specs=in_specs, out_specs=out_specs, check_vma=False)
```

profile of v0, /device:TPU:2, one launch (start us, length us, event | category | flops | bytes accessed | tf_op | source)
XLA Modules:
  0.0 187.8 jit_solution(73576553824263236)
XLA Ops:
  0.0 0.2 negate_convert_fusion.2
  0.5 0.3 negate_convert_fusion
  0.7 0.3 multiply_convert_fusion.1
  1.0 0.3 multiply_convert_fusion.3
  1.3 1.1 convert_bitcast_fusion.1
  2.7 0.2 fusion.84
  2.9 0.3 convolution_bitcast_fusion.1
  3.2 0.2 subtract_convert_fusion
  3.4 0.3 fusion.38
  3.8 5.6 %copy.128 = bf16[2,16,128,64]{1,0,3,2:T(2,128)(2,1)} copy(bf16[2,16,128,64]{2,3,0,1:T(8,128)(2,1)S(1)} %fusion.38) | data formatting | bytes 1048576 | tf_op jit(solution)/shard_map/convert_element_type | solution.py:70
  9.3 6.5 %reshape.594 = bf16[8,2,16384]{2,1,0:T(2,128)(2,1)} reshape(bf16[8192,2,16]{2,1,0:T(2,128)(2,1)} %bitcast.278) | data formatting | bytes 1048576
  15.8 4.9 %all-to-all-start = ((bf16[8,2,16384]{2,1,0:T(2,128)(2,1)}), bf16[8,2,16384]{2,1,0:T(2,128)(2,1)S(1)}, u32[]{:S(2)}, u32[]{:S(2)}) async-start(bf16[8,2,16384]{2,1,0:T(2,128)(2,1)} %reshape.594), calls=%async_computation | async-start | bytes 1048576 | tf_op jit(solution)/shard_map/all_to_all | solution.py:128
  20.7 0.2 convert_reduce_fusion
  21.0 15.0 %all-to-all-done = bf16[8,2,16384]{2,1,0:T(2,128)(2,1)S(1)} async-done(((bf16[8,2,16384]{2,1,0:T(2,128)(2,1)}), bf16[8,2,16384]{2,1,0:T(2,128)(2,1)S(1)}, u32[]{:S(2)}, u32[]{:S(2)}) %all-to-all-start) | async-done | bytes 524320 | tf_op jit(solution)/shard_map/all_to_all | solution.py:128
  36.0 4.1 %reshape.595 = bf16[8192,2,16]{2,1,0:T(2,128)(2,1)} reshape(bf16[8,2,16384]{2,1,0:T(2,128)(2,1)S(1)} %all-to-all-done) | data formatting | bytes 1048576
  40.1 9.0 %copy.130 = bf16[2,16,8,1024]{3,1,2,0:T(8,128)(2,1)S(1)} copy(bf16[2,16,8,1024]{1,0,3,2:T(2,128)(2,1)} %bitcast.279) | data formatting | bytes 1048576 | tf_op jit(solution)/shard_map/all_to_all | solution.py:128
  49.0 0.3 convolution_bitcast_fusion.3
  49.4 0.2 fusion.56
  49.6 0.3 fusion.37
  50.0 0.5 convolution_convert_fusion.2
  50.5 2.0 %copy.79 = bf16[8,2,2,128,128]{4,1,3,2,0:T(2,128)(2,1)} copy(bf16[8,2,2,128,128]{4,1,0,3,2:T(2,128)(2,1)S(1)} %bitcast.281) | data formatting | bytes 2097152 | tf_op jit(solution)/shard_map/reshape | solution.py:153
  52.5 3.6 %all-to-all-start.1 = ((bf16[8,2,2,128,128]{4,1,3,2,0:T(2,128)(2,1)}), bf16[8,2,2,128,128]{4,1,3,2,0:T(2,128)(2,1)S(1)}, u32[]{:S(2)}, u32[]{:S(2)}) async-start(bf16[8,2,2,128,128]{4,1,3,2,0:T(2,128)(2,1)} %copy.79), calls=%async_computation.1 | async-start | bytes 2097152 | tf_op jit(solution)/shard_map/all_to_all | solution.py:154
  56.3 2.8 %fusion.39 = bf16[2,8,128,128]{3,1,2,0:T(8,128)(2,1)S(1)} fusion(f32[8]{0:T(128)S(1)} %add_multiply_fusion, f32[16384]{0:T(1024)S(1)} %subtract_bitcast_fusion, s32[16]{0:T(128)S(1)} %select_reduce_fusion), kind=kOutput, calls=%fused_computation.74 | convolution fusion | flops 9830528 | bytes 589920 | tf_op jit(solution)/shard_map/dot_general | solution.py:89
  59.2 23.4 %all-to-all-done.1 = bf16[8,2,2,128,128]{4,1,3,2,0:T(2,128)(2,1)S(1)} async-done(((bf16[8,2,2,128,128]{4,1,3,2,0:T(2,128)(2,1)}), bf16[8,2,2,128,128]{4,1,3,2,0:T(2,128)(2,1)S(1)}, u32[]{:S(2)}, u32[]{:S(2)}) %all-to-all-start.1) | async-done | bytes 1048608 | tf_op jit(solution)/shard_map/all_to_all | solution.py:154
  82.6 0.7 copy.80
  83.3 0.6 convolution_convert_fusion.1
  83.9 0.5 fusion.35
  84.4 0.8 collective-permute-start
  85.2 1.5 collective-permute-start.1
  86.7 23.6 %collective-permute-done = bf16[16,2,128,128]{2,3,1,0:T(8,128)(2,1)S(1)} collective-permute-done((bf16[16,2,128,128]{2,3,1,0:T(8,128)(2,1)S(1)}, bf16[16,2,128,128]{2,3,1,0:T(8,128)(2,1)S(1)}, u32[]{:S(2)}, u32[]{:S(2)}) %collective-permute-start) | collective-permute-done | bytes 1048608 | tf_op jit(solution)/shard_map/ppermute | solution.py:17
  110.3 21.7 %collective-permute-done.1 = bf16[16,2,128,128]{2,3,1,0:T(8,128)(2,1)S(1)} collective-permute-done((bf16[16,2,128,128]{2,3,1,0:T(8,128)(2,1)S(1)}, bf16[16,2,128,128]{2,3,1,0:T(8,128)(2,1)S(1)}, u32[]{:S(2)}, u32[]{:S(2)}) %collective-permute-start.1) | collective-permute-done | bytes 1048608 | tf_op jit(solution)/shard_map/ppermute | solution.py:17
  132.0 1.0 fusion.45
  133.2 3.4 %convolution_bitcast_fusion = f32[16,2,2,128,128]{3,4,1,0,2:T(8,128)} fusion(bf16[1,2,128,128]{3,2,1,0:T(8,128)(2,1)S(1)} %get-tuple-element.44, bf16[1,2,128,128]{3,2,1,0:T(8,128)(2,1)S(1)} %get-tuple-element.43, bf16[16,1,2,128,128]{3,4,2,0,1:T(8,128)(2,1)S(1)} %maximum_bitcast_fusion.2, bf16[16,1,2,128,128]{3,4,2,0,1:T(8,128)(2,1)S(1)} %maximum_bitcast_fusion.1), kind=kOutput, calls=%fused_computation.5 | convolution fusion | flops 1076363264 | bytes 6422528 | tf_op jit(solution)/shard_map/npeuj,cvej->npcuv/dot_general | solution.py:48
  136.7 2.5 %fusion.96 = f32[16,2,128,128]{2,3,1,0:T(8,128)S(1)} fusion(f32[16,2,2,128,128]{3,4,1,0,2:T(8,128)} %convolution_bitcast_fusion), kind=kLoop, calls=%fused_computation.151 | loop fusion | flops 1572864 | bytes 6291456 | tf_op jit(solution)/shard_map/add | solution.py:109
  139.2 3.0 %slice_bitcast_fusion.5 = (f32[16,2,1,127,128]{3,4,1,0,2:T(8,128)}, f32[16,2,1,127,128]{3,4,1,0,2:T(8,128)}, f32[16,2,127,128]{2,3,1,0:T(8,128)S(1)}, f32[16,2,127,128]{2,3,1,0:T(8,128)S(1)}) fusion(f32[16,2,128,128]{2,3,1,0:T(8,128)S(1)} %fusion.96), kind=kLoop, calls=%fused_computation.281 | loop fusion | bytes 12484608 | tf_op jit(solution)/shard_map/jit(_roll_static)/concatenate | solution.py:113
  142.2 0.7 fusion.191
  143.1 0.5 copy-done.2
  143.6 3.2 %slice_maximum_fusion.3 = (f32[16,2,128,127]{2,3,1,0:T(8,128)}, f32[16,2,128,127]{2,3,1,0:T(8,128)}) fusion(f32[16,2,1,128]{2,3,1,0:T(8,128)S(1)} %get-tuple-element.25, f32[16,2,127,128]{2,3,1,0:T(8,128)S(1)} %get-tuple-element.24), kind=kLoop, calls=%fused_computation.10 | loop fusion | flops 1040384 | bytes 6258688 | tf_op jit(solution)/shard_map/jit(_roll_static)/concatenate | solution.py:113
  146.9 3.3 %slice_maximum_fusion.1 = (f32[16,2,128,127]{2,3,1,0:T(8,128)}, f32[16,2,128,127]{2,3,1,0:T(8,128)}) fusion(f32[16,2,127,128]{2,3,1,0:T(8,128)S(1)} %get-tuple-element.23, f32[16,2,1,128]{2,3,1,0:T(8,128)S(1)} %get-tuple-element.26), kind=kLoop, calls=%fused_computation.8 | loop fusion | flops 1040384 | bytes 6258688 | tf_op jit(solution)/shard_map/jit(_roll_static)/concatenate | solution.py:113
  150.2 4.0 %fusion.189 = (f32[16,2,128,127]{2,3,1,0:T(8,128)}, f32[16,2,1,128,127]{3,4,1,0,2:T(8,128)}, f32[16,2,1,128,127]{3,4,1,0,2:T(8,128)}, f32[16,2,128,127]{2,3,1,0:T(8,128)}) fusion(f32[16,2,128,128]{2,3,1,0:T(8,128)S(1)} %fusion.96), kind=kLoop, calls=%fused_computation.282 | loop fusion | bytes 12484608 | tf_op jit(solution)/shard_map/jit(_roll_static)/slice | solution.py:113
  154.3 2.2 %copy.99 = f32[16,2,1,128]{3,0,2,1:T(8,128)S(1)} copy(f32[16,2,1,128]{2,3,1,0:T(8,128)} %copy-done) | data formatting | bytes 32768 | tf_op jit(solution)/shard_map/jit(_roll_static)/slice | solution.py:113
  156.5 0.6 copy.88
  157.1 9.2 %fusion.23 = f32[16,2]{1,0:T(8,128)S(1)} fusion(f32[16,2,128,127]{2,3,1,0:T(8,128)} %get-tuple-element.10, f32[16,2,128,1]{2,3,1,0:T(1,128)S(1)} %get-tuple-element.12, f32[16,2,128,1]{2,3,1,0:T(1,128)S(1)} %get-tuple-element.11, f32[16,2,128,127]{2,3,1,0:T(8,128)} %get-tuple-element.9, f32[16,2,128,127]{2,3,1,0:T(8,128)} %get-tuple-element.16, ...), kind=kLoop, calls=%fused_computation.39 | loop fusion | flops 11010016 | bytes 20971648 | tf_op jit(solution)/shard_map/reduce_sum | solution.py:115
  166.3 1.9 %copy.100 = f32[16,2,1,1,128]{3,4,1,0,2:T(8,128)} copy(f32[16,2,1,1,128]{4,0,3,2,1:T(8,128)S(1)} %bitcast.293) | data formatting | bytes 32768 | tf_op jit(solution)/shard_map/jit(_roll_static)/concatenate | solution.py:113
  168.2 2.0 %copy.89 = f32[16,2,1,1,128]{3,4,1,0,2:T(8,128)} copy(f32[16,2,1,1,128]{4,0,3,2,1:T(8,128)S(1)} %bitcast.292) | data formatting | bytes 32768 | tf_op jit(solution)/shard_map/jit(_roll_static)/concatenate | solution.py:113
  170.3 10.6 %sqrt_bitcast_fusion = f32[16,2,128,128]{2,3,1,0:T(8,128)} fusion(f32[16,2,1,128,127]{3,4,1,0,2:T(8,128)} %bitcast.277, f32[16,2,1,128,1]{3,4,1,0,2:T(1,128)S(1)} %bitcast.289, f32[16,2,1,127,128]{3,4,1,0,2:T(8,128)} %get-tuple-element.22, f32[16,2,1,1,128]{3,4,1,0,2:T(8,128)} %copy.100, f32[16,2,1,128,1]{3,4,1,0,2:T(1,128)S(1)} %bitcast.288, ...), kind=kLoop, calls=%fused_computation.38 | loop fusion | flops 11010048 | bytes 23068800 | tf_op jit(solution)/shard_map/mul | solution.py:117
  180.8 4.3 %fusion.24 = bf16[1,16,2,2,128,128]{4,5,2,1,3,0:T(8,128)(2,1)S(1)} fusion(bf16[1,2,128,128]{3,2,1,0:T(8,128)(2,1)S(1)} %get-tuple-element.45, bf16[1,2,128,128]{3,2,1,0:T(8,128)(2,1)S(1)} %get-tuple-element.46, f32[16,2,2,128,128]{3,4,1,0,2:T(8,128)} %convolution_bitcast_fusion, f32[16,2,128,128]{2,3,1,0:T(8,128)} %sqrt_bitcast_fusion), kind=kOutput, calls=%fused_computation.54 | convolution fusion | flops 1078460416 | bytes 8519680 | tf_op jit(solution)/shard_map/npeuj,cvej->npcuv/dot_general | solution.py:48
  185.2 2.6 %copy.106 = bf16[1,16,2,2,128,128]{5,4,3,2,1,0:T(8,128)(2,1)} copy(bf16[1,16,2,2,128,128]{4,5,2,1,3,0:T(8,128)(2,1)S(1)} %fusion.24) | data formatting | bytes 4194304 | tf_op jit(solution)/shard_map/broadcast_in_dim | solution.py:170
  (39 shorter events, 1.6 us)
Async XLA Ops:
  0.0 2.6 %copy-start.5 = (f32[2,8192]{1,0:T(2,128)S(1)}, f32[2,8192]{1,0:T(2,128)}, u32[]{:S(2)}) copy-start(f32[2,8192]{1,0:T(2,128)} %param.7) | copy-start | bytes 196612
  9.3 11.4 %copy-start.6 = (s32[1,64]{1,0:T(1,128)S(1)}, s32[1,64]{1,0:T(1,128)}, u32[]{:S(2)}) copy-start(s32[1,64]{1,0:T(1,128)} %param.9) | copy-start | bytes 772
  15.8 20.2 %all-to-all-start = ((bf16[8,2,16384]{2,1,0:T(2,128)(2,1)}), bf16[8,2,16384]{2,1,0:T(2,128)(2,1)S(1)}, u32[]{:S(2)}, u32[]{:S(2)}) async-start(bf16[8,2,16384]{2,1,0:T(2,128)(2,1)} %reshape.594), calls=%async_computation | async-start | bytes 1048576 | tf_op jit(solution)/shard_map/all_to_all | solution.py:128
  40.1 9.3 %copy-start.4 = (bf16[2,128,1024]{2,1,0:T(8,128)(2,1)S(1)}, bf16[2,128,1024]{2,1,0:T(8,128)(2,1)}, u32[]{:S(2)}) copy-start(bf16[2,128,1024]{2,1,0:T(8,128)(2,1)} %param.8) | copy-start | bytes 1572868
  50.5 5.6 %copy-start.7 = (s32[1,64]{1,0:T(1,128)S(1)}, s32[1,64]{1,0:T(1,128)}, u32[]{:S(2)}) copy-start(s32[1,64]{1,0:T(1,128)} %param.10) | copy-start | bytes 772
  50.5 5.6 %copy-start.8 = (s32[1,64]{1,0:T(1,128)S(1)}, s32[1,64]{1,0:T(1,128)}, u32[]{:S(2)}) copy-start(s32[1,64]{1,0:T(1,128)} %param.11) | copy-start | bytes 772
  52.5 30.1 %all-to-all-start.1 = ((bf16[8,2,2,128,128]{4,1,3,2,0:T(2,128)(2,1)}), bf16[8,2,2,128,128]{4,1,3,2,0:T(2,128)(2,1)S(1)}, u32[]{:S(2)}, u32[]{:S(2)}) async-start(bf16[8,2,2,128,128]{4,1,3,2,0:T(2,128)(2,1)} %copy.79), calls=%async_computation.1 | async-start | bytes 2097152 | tf_op jit(solution)/shard_map/all_to_all | solution.py:154
  84.4 25.8 %collective-permute-start = (bf16[16,2,128,128]{2,3,1,0:T(8,128)(2,1)S(1)}, bf16[16,2,128,128]{2,3,1,0:T(8,128)(2,1)S(1)}, u32[]{:S(2)}, u32[]{:S(2)}) collective-permute-start(bf16[16,2,128,128]{2,3,1,0:T(8,128)(2,1)S(1)} %fusion.35), channel_id=1, source_target_pairs={{0,24},{8,0},{16,8},{24,16},{1,25},{9,1},{17,9},{25,17},{2,26},{10... | collective-permute-start | bytes 3145736 | tf_op jit(solution)/shard_map/ppermute | solution.py:17
  85.2 46.8 %collective-permute-start.1 = (bf16[16,2,128,128]{2,3,1,0:T(8,128)(2,1)S(1)}, bf16[16,2,128,128]{2,3,1,0:T(8,128)(2,1)S(1)}, u32[]{:S(2)}, u32[]{:S(2)}) collective-permute-start(bf16[16,2,128,128]{2,3,1,0:T(8,128)(2,1)S(1)} %fusion.35), channel_id=1, source_target_pairs={{0,16},{8,24},{16,0},{24,8},{1,17},{9,25},{17,1},{25,9},{2,18},{10... | collective-permute-start | bytes 3145736 | tf_op jit(solution)/shard_map/ppermute | solution.py:17
  142.2 1.4 copy-start.2
  142.2 4.7 %copy-start.1 = (f32[16,2,127,128]{2,3,1,0:T(8,128)}, f32[16,2,127,128]{2,3,1,0:T(8,128)S(1)}, u32[]{:S(2)}) copy-start(f32[16,2,127,128]{2,3,1,0:T(8,128)S(1)} %get-tuple-element.23) | copy-start | bytes 6242308
  143.0 4.0 %copy-start = (f32[16,2,1,128]{2,3,1,0:T(8,128)}, f32[16,2,1,128]{2,3,1,0:T(8,128)S(1)}, u32[]{:S(2)}) copy-start(f32[16,2,1,128]{2,3,1,0:T(8,128)S(1)} %get-tuple-element.26) | copy-start | bytes 49156
  166.3 4.0 %copy-start.3 = (f32[16,2,128,127]{2,3,1,0:T(8,128)S(1)}, f32[16,2,128,127]{2,3,1,0:T(8,128)}, u32[]{:S(2)}) copy-start(f32[16,2,128,127]{2,3,1,0:T(8,128)} %get-tuple-element.5) | copy-start | bytes 6242308
where the time goes:
time: 188 us
  waiting for transfers between devices  83.7 us (45%)
  local copies, waits for them, and re-layouts  46 us (24%)
  other arithmetic  33.5 us (18%)
  matrix products  13.5 us (7%)
  starting transfers between devices  10.7 us (6%)
    ppermute x2, waiting for transfers between devices, passed_along(): return lax.ppermute(value, axis, pairs)  45.3 us
    all_to_all x1, waiting for transfers between devices, body(): lax.all_to_all(outbox, 'shard', split_axis=0, concat_axis=0, tiled=True)  23.4 us
    all_to_all x1, waiting for transfers between devices, body(): lax.all_to_all(compressed, 'shard', split_axis=2, concat_axis=1, tiled=True)  15 us
    unnamed x24, local copies, waits for them, and re-layouts  11.4 us
    dot_general x9, matrix products, bdot(): return jnp.einsum(form, left, right, preferred_element_type=jnp.float32)  10.7 us
    mul x1, other arithmetic, goldstein(): weighted = (spectrum * weight[:, :, None]).astype(jnp.bfloat16)  10.6 us
    reduce_sum x1, other arithmetic, goldstein(): level = jnp.mean(smooth, axis=(-2, -1), keepdims=True)  9.16 us
    all_to_all x1, local copies, waits for them, and re-layouts, body(): lax.all_to_all(compressed, 'shard', split_axis=2, concat_axis=1, tiled=True)  8.96 us
  transfers between devices with their start and end apart: 4, of which 4 were waited for; matrix products, arithmetic and copies ran while one was open for 2% of the time, Pallas kernels for 0%

commit v1 on v0

--- a/solution.py
+++ b/solution.py
@@ -125,7 +125,9 @@
     capacity = min(2 * BLK_DEV, shards * most)
     outgoing = shards * most
     compressed = range_compress(echo_spectra[0], range_reference)
-    columns = lax.all_to_all(compressed, "shard", split_axis=2, concat_axis=1, tiled=True)
+    parts = jnp.split(compressed, lax.axis_size("shard"), axis=2)
+    incoming = lax.all_to_all(jnp.stack(parts), "shard", 0, 0)
+    columns = jnp.concatenate(incoming, axis=1)
     image = azimuth_focus(columns, azimuth_reference)
     row_blocks = image.shape[1] // BLK
     col_blocks = image.shape[2] // BLK

time: 188 us -> 169 us (0.90)
  local copies, waits for them, and re-layouts: 46 us -> 27.3 us
    all_to_all x1 -> x0, local copies, waits for them, and re-layouts: 8.96 us -> none  [body(): lax.all_to_all(compressed, 'shard', split_axis=2, concat_axis=1, tiled=True)]
    unnamed x24 -> x29, local copies, waits for them, and re-layouts: 11.4 us -> 5.34 us
    convert_element_type x1 -> x2, local copies, waits for them, and re-layouts: 5.57 us -> 1.3 us  [range_compress(): return second.reshape(2, count, RNG).astype(jnp.bfloat16)]
where the time goes in v1:
time: 169 us
  waiting for transfers between devices  83.7 us (50%)
  other arithmetic  33.5 us (20%)
  local copies, waits for them, and re-layouts  27.3 us (16%)
  matrix products  13.5 us (8%)
  starting transfers between devices  10.7 us (6%)
    ppermute x2, waiting for transfers between devices, passed_along(): return lax.ppermute(value, axis, pairs)  45.3 us
    all_to_all x1, waiting for transfers between devices, body(): lax.all_to_all(outbox, 'shard', split_axis=0, concat_axis=0, tiled=True)  23.4 us
    all_to_all x1, waiting for transfers between devices, body(): incoming = lax.all_to_all(jnp.stack(parts), 'shard', 0, 0)  15 us
    dot_general x9, matrix products, bdot(): return jnp.einsum(form, left, right, preferred_element_type=jnp.float32)  10.7 us
    mul x1, other arithmetic, goldstein(): weighted = (spectrum * weight[:, :, None]).astype(jnp.bfloat16)  10.6 us
    reduce_sum x1, other arithmetic, goldstein(): level = jnp.mean(smooth, axis=(-2, -1), keepdims=True)  9.16 us
    slice x5, local copies, waits for them, and re-layouts, goldstein(): smooth = smooth + jnp.roll(power, (down, across), axis=(-2, -1))  7.63 us
    concatenate x3, local copies, waits for them, and re-layouts, goldstein(): smooth = smooth + jnp.roll(power, (down, across), axis=(-2, -1))  6.95 us
  transfers between devices with their start and end apart: 4, of which 4 were waited for; matrix products, arithmetic and copies ran while one was open for 2% of the time, Pallas kernels for 0%

profile of v1, /device:TPU:2, one launch (start us, length us, event | category | flops | bytes accessed | tf_op | source)
XLA Modules:
  0.0 169.1 jit_solution(16456775039508118923)
XLA Ops:
  0.5 0.3 negate_convert_fusion
  0.7 0.3 multiply_convert_fusion.1
  1.3 1.1 convert_bitcast_fusion.1
  2.9 0.3 convolution_bitcast_fusion.1
  3.4 0.3 fusion.38
  3.8 0.5 copy.80
  4.3 0.8 convert_element_type.270
  5.1 0.6 fusion.136
  5.7 0.6 fusion.135
  6.3 0.6 fusion.134
  7.0 0.6 fusion.133
  7.6 0.6 fusion.132
  8.2 0.6 fusion.131
  8.9 0.6 fusion.130
  9.5 0.6 fusion.129
  10.2 4.9 %all-to-all-start = ((bf16[8,2,16,1024]{3,2,1,0:T(8,128)(2,1)}), bf16[8,2,16,1024]{3,2,1,0:T(8,128)(2,1)S(1)}, u32[]{:S(2)}, u32[]{:S(2)}) async-start(bf16[8,2,16,1024]{3,2,1,0:T(8,128)(2,1)} %fusion.129), calls=%async_computation | async-start | bytes 1048576 | tf_op jit(solution)/shard_map/all_to_all | solution.py:129
  15.3 15.0 %all-to-all-done = bf16[8,2,16,1024]{3,2,1,0:T(8,128)(2,1)S(1)} async-done(((bf16[8,2,16,1024]{3,2,1,0:T(8,128)(2,1)}), bf16[8,2,16,1024]{3,2,1,0:T(8,128)(2,1)S(1)}, u32[]{:S(2)}, u32[]{:S(2)}) %all-to-all-start) | async-done | bytes 524320 | tf_op jit(solution)/shard_map/all_to_all | solution.py:129
  30.4 0.3 convolution_bitcast_fusion.3
  30.9 0.3 fusion.37
  31.3 0.5 convolution_convert_fusion.2
  31.9 2.0 %copy.82 = bf16[8,2,2,128,128]{4,1,3,2,0:T(2,128)(2,1)} copy(bf16[8,2,2,128,128]{4,1,0,3,2:T(2,128)(2,1)S(1)} %bitcast.307) | data formatting | bytes 2097152 | tf_op jit(solution)/shard_map/reshape | solution.py:155
  33.9 3.6 %all-to-all-start.1 = ((bf16[8,2,2,128,128]{4,1,3,2,0:T(2,128)(2,1)}), bf16[8,2,2,128,128]{4,1,3,2,0:T(2,128)(2,1)S(1)}, u32[]{:S(2)}, u32[]{:S(2)}) async-start(bf16[8,2,2,128,128]{4,1,3,2,0:T(2,128)(2,1)} %copy.82), calls=%async_computation.1 | async-start | bytes 2097152 | tf_op jit(solution)/shard_map/all_to_all | solution.py:156
  37.6 2.8 %fusion.39 = bf16[2,8,128,128]{3,1,2,0:T(8,128)(2,1)S(1)} fusion(f32[8]{0:T(128)S(1)} %add_multiply_fusion, f32[16384]{0:T(1024)S(1)} %subtract_bitcast_fusion, s32[16]{0:T(128)S(1)} %select_reduce_fusion), kind=kOutput, calls=%fused_computation.74 | convolution fusion | flops 9830528 | bytes 589920 | tf_op jit(solution)/shard_map/dot_general | solution.py:89
  40.6 23.4 %all-to-all-done.1 = bf16[8,2,2,128,128]{4,1,3,2,0:T(2,128)(2,1)S(1)} async-done(((bf16[8,2,2,128,128]{4,1,3,2,0:T(2,128)(2,1)}), bf16[8,2,2,128,128]{4,1,3,2,0:T(2,128)(2,1)S(1)}, u32[]{:S(2)}, u32[]{:S(2)}) %all-to-all-start.1) | async-done | bytes 1048608 | tf_op jit(solution)/shard_map/all_to_all | solution.py:156
  63.9 0.7 copy.83
  64.7 0.6 convolution_convert_fusion.1
  65.3 0.5 fusion.35
  65.8 0.8 collective-permute-start
  66.5 1.5 collective-permute-start.1
  68.1 23.6 %collective-permute-done = bf16[16,2,128,128]{2,3,1,0:T(8,128)(2,1)S(1)} collective-permute-done((bf16[16,2,128,128]{2,3,1,0:T(8,128)(2,1)S(1)}, bf16[16,2,128,128]{2,3,1,0:T(8,128)(2,1)S(1)}, u32[]{:S(2)}, u32[]{:S(2)}) %collective-permute-start) | collective-permute-done | bytes 1048608 | tf_op jit(solution)/shard_map/ppermute | solution.py:17
  91.6 21.7 %collective-permute-done.1 = bf16[16,2,128,128]{2,3,1,0:T(8,128)(2,1)S(1)} collective-permute-done((bf16[16,2,128,128]{2,3,1,0:T(8,128)(2,1)S(1)}, bf16[16,2,128,128]{2,3,1,0:T(8,128)(2,1)S(1)}, u32[]{:S(2)}, u32[]{:S(2)}) %collective-permute-start.1) | collective-permute-done | bytes 1048608 | tf_op jit(solution)/shard_map/ppermute | solution.py:17
  113.3 1.0 fusion.45
  114.6 3.4 %convolution_bitcast_fusion = f32[16,2,2,128,128]{3,4,1,0,2:T(8,128)} fusion(bf16[1,2,128,128]{3,2,1,0:T(8,128)(2,1)S(1)} %get-tuple-element.44, bf16[1,2,128,128]{3,2,1,0:T(8,128)(2,1)S(1)} %get-tuple-element.43, bf16[16,1,2,128,128]{3,4,2,0,1:T(8,128)(2,1)S(1)} %maximum_bitcast_fusion.2, bf16[16,1,2,128,128]{3,4,2,0,1:T(8,128)(2,1)S(1)} %maximum_bitcast_fusion.1), kind=kOutput, calls=%fused_computation.5 | convolution fusion | flops 1076363264 | bytes 6422528 | tf_op jit(solution)/shard_map/npeuj,cvej->npcuv/dot_general | solution.py:48
  118.0 2.5 %fusion.96 = f32[16,2,128,128]{2,3,1,0:T(8,128)S(1)} fusion(f32[16,2,2,128,128]{3,4,1,0,2:T(8,128)} %convolution_bitcast_fusion), kind=kLoop, calls=%fused_computation.151 | loop fusion | flops 1572864 | bytes 6291456 | tf_op jit(solution)/shard_map/add | solution.py:109
  120.6 3.0 %slice_bitcast_fusion.13 = (f32[16,2,1,127,128]{3,4,1,0,2:T(8,128)}, f32[16,2,1,127,128]{3,4,1,0,2:T(8,128)}, f32[16,2,127,128]{2,3,1,0:T(8,128)S(1)}, f32[16,2,127,128]{2,3,1,0:T(8,128)S(1)}) fusion(f32[16,2,128,128]{2,3,1,0:T(8,128)S(1)} %fusion.96), kind=kLoop, calls=%fused_computation.297 | loop fusion | bytes 12484608 | tf_op jit(solution)/shard_map/jit(_roll_static)/concatenate | solution.py:113
  123.6 0.7 fusion.199
  124.5 0.5 copy-done.2
  124.9 3.2 %slice_maximum_fusion.3 = (f32[16,2,128,127]{2,3,1,0:T(8,128)}, f32[16,2,128,127]{2,3,1,0:T(8,128)}) fusion(f32[16,2,1,128]{2,3,1,0:T(8,128)S(1)} %get-tuple-element.25, f32[16,2,127,128]{2,3,1,0:T(8,128)S(1)} %get-tuple-element.24), kind=kLoop, calls=%fused_computation.10 | loop fusion | flops 1040384 | bytes 6258688 | tf_op jit(solution)/shard_map/jit(_roll_static)/concatenate | solution.py:113
  128.3 3.3 %slice_maximum_fusion.1 = (f32[16,2,128,127]{2,3,1,0:T(8,128)}, f32[16,2,128,127]{2,3,1,0:T(8,128)}) fusion(f32[16,2,127,128]{2,3,1,0:T(8,128)S(1)} %get-tuple-element.23, f32[16,2,1,128]{2,3,1,0:T(8,128)S(1)} %get-tuple-element.26), kind=kLoop, calls=%fused_computation.8 | loop fusion | flops 1040384 | bytes 6258688 | tf_op jit(solution)/shard_map/jit(_roll_static)/concatenate | solution.py:113
  131.6 4.0 %fusion.197 = (f32[16,2,128,127]{2,3,1,0:T(8,128)}, f32[16,2,1,128,127]{3,4,1,0,2:T(8,128)}, f32[16,2,1,128,127]{3,4,1,0,2:T(8,128)}, f32[16,2,128,127]{2,3,1,0:T(8,128)}) fusion(f32[16,2,128,128]{2,3,1,0:T(8,128)S(1)} %fusion.96), kind=kLoop, calls=%fused_computation.298 | loop fusion | bytes 12484608 | tf_op jit(solution)/shard_map/jit(_roll_static)/slice | solution.py:113
  135.6 2.2 %copy.102 = f32[16,2,1,128]{3,0,2,1:T(8,128)S(1)} copy(f32[16,2,1,128]{2,3,1,0:T(8,128)} %copy-done) | data formatting | bytes 32768 | tf_op jit(solution)/shard_map/jit(_roll_static)/slice | solution.py:113
  137.8 0.6 copy.91
  138.5 9.2 %fusion.23 = f32[16,2]{1,0:T(8,128)S(1)} fusion(f32[16,2,128,127]{2,3,1,0:T(8,128)} %get-tuple-element.10, f32[16,2,128,1]{2,3,1,0:T(1,128)S(1)} %get-tuple-element.12, f32[16,2,128,1]{2,3,1,0:T(1,128)S(1)} %get-tuple-element.11, f32[16,2,128,127]{2,3,1,0:T(8,128)} %get-tuple-element.9, f32[16,2,128,127]{2,3,1,0:T(8,128)} %get-tuple-element.16, ...), kind=kLoop, calls=%fused_computation.39 | loop fusion | flops 11010016 | bytes 20971648 | tf_op jit(solution)/shard_map/reduce_sum | solution.py:115
  147.7 1.9 %copy.103 = f32[16,2,1,1,128]{3,4,1,0,2:T(8,128)} copy(f32[16,2,1,1,128]{4,0,3,2,1:T(8,128)S(1)} %bitcast.320) | data formatting | bytes 32768 | tf_op jit(solution)/shard_map/jit(_roll_static)/concatenate | solution.py:113
  149.6 2.0 %copy.92 = f32[16,2,1,1,128]{3,4,1,0,2:T(8,128)} copy(f32[16,2,1,1,128]{4,0,3,2,1:T(8,128)S(1)} %bitcast.319) | data formatting | bytes 32768 | tf_op jit(solution)/shard_map/jit(_roll_static)/concatenate | solution.py:113
  151.6 10.6 %sqrt_bitcast_fusion = f32[16,2,128,128]{2,3,1,0:T(8,128)} fusion(f32[16,2,1,128,127]{3,4,1,0,2:T(8,128)} %bitcast.305, f32[16,2,1,128,1]{3,4,1,0,2:T(1,128)S(1)} %bitcast.316, f32[16,2,1,127,128]{3,4,1,0,2:T(8,128)} %get-tuple-element.22, f32[16,2,1,1,128]{3,4,1,0,2:T(8,128)} %copy.103, f32[16,2,1,128,1]{3,4,1,0,2:T(1,128)S(1)} %bitcast.315, ...), kind=kLoop, calls=%fused_computation.38 | loop fusion | flops 11010048 | bytes 23068800 | tf_op jit(solution)/shard_map/mul | solution.py:117
  162.2 4.3 %fusion.24 = bf16[1,16,2,2,128,128]{4,5,2,1,3,0:T(8,128)(2,1)S(1)} fusion(bf16[1,2,128,128]{3,2,1,0:T(8,128)(2,1)S(1)} %get-tuple-element.45, bf16[1,2,128,128]{3,2,1,0:T(8,128)(2,1)S(1)} %get-tuple-element.46, f32[16,2,2,128,128]{3,4,1,0,2:T(8,128)} %convolution_bitcast_fusion, f32[16,2,128,128]{2,3,1,0:T(8,128)} %sqrt_bitcast_fusion), kind=kOutput, calls=%fused_computation.54 | convolution fusion | flops 1078460416 | bytes 8519680 | tf_op jit(solution)/shard_map/npeuj,cvej->npcuv/dot_general | solution.py:48
  166.5 2.6 %copy.109 = bf16[1,16,2,2,128,128]{5,4,3,2,1,0:T(8,128)(2,1)} copy(bf16[1,16,2,2,128,128]{4,5,2,1,3,0:T(8,128)(2,1)S(1)} %fusion.24) | data formatting | bytes 4194304 | tf_op jit(solution)/shard_map/broadcast_in_dim | solution.py:172
  (46 shorter events, 2.7 us)
Async XLA Ops:
  0.0 2.6 %copy-start.5 = (f32[2,8192]{1,0:T(2,128)S(1)}, f32[2,8192]{1,0:T(2,128)}, u32[]{:S(2)}) copy-start(f32[2,8192]{1,0:T(2,128)} %param.7) | copy-start | bytes 196612
  4.2 10.8 %copy-start.6 = (s32[1,64]{1,0:T(1,128)S(1)}, s32[1,64]{1,0:T(1,128)}, u32[]{:S(2)}) copy-start(s32[1,64]{1,0:T(1,128)} %param.9) | copy-start | bytes 772
  8.2 22.5 %copy-start.4 = (bf16[2,128,1024]{2,1,0:T(8,128)(2,1)S(1)}, bf16[2,128,1024]{2,1,0:T(8,128)(2,1)}, u32[]{:S(2)}) copy-start(bf16[2,128,1024]{2,1,0:T(8,128)(2,1)} %param.8) | copy-start | bytes 1572868
  10.2 20.2 %all-to-all-start = ((bf16[8,2,16,1024]{3,2,1,0:T(8,128)(2,1)}), bf16[8,2,16,1024]{3,2,1,0:T(8,128)(2,1)S(1)}, u32[]{:S(2)}, u32[]{:S(2)}) async-start(bf16[8,2,16,1024]{3,2,1,0:T(8,128)(2,1)} %fusion.129), calls=%async_computation | async-start | bytes 1048576 | tf_op jit(solution)/shard_map/all_to_all | solution.py:129
  31.9 5.6 %copy-start.7 = (s32[1,64]{1,0:T(1,128)S(1)}, s32[1,64]{1,0:T(1,128)}, u32[]{:S(2)}) copy-start(s32[1,64]{1,0:T(1,128)} %param.10) | copy-start | bytes 772
  31.9 5.6 %copy-start.8 = (s32[1,64]{1,0:T(1,128)S(1)}, s32[1,64]{1,0:T(1,128)}, u32[]{:S(2)}) copy-start(s32[1,64]{1,0:T(1,128)} %param.11) | copy-start | bytes 772
  33.9 30.1 %all-to-all-start.1 = ((bf16[8,2,2,128,128]{4,1,3,2,0:T(2,128)(2,1)}), bf16[8,2,2,128,128]{4,1,3,2,0:T(2,128)(2,1)S(1)}, u32[]{:S(2)}, u32[]{:S(2)}) async-start(bf16[8,2,2,128,128]{4,1,3,2,0:T(2,128)(2,1)} %copy.82), calls=%async_computation.1 | async-start | bytes 2097152 | tf_op jit(solution)/shard_map/all_to_all | solution.py:156
  65.8 25.8 %collective-permute-start = (bf16[16,2,128,128]{2,3,1,0:T(8,128)(2,1)S(1)}, bf16[16,2,128,128]{2,3,1,0:T(8,128)(2,1)S(1)}, u32[]{:S(2)}, u32[]{:S(2)}) collective-permute-start(bf16[16,2,128,128]{2,3,1,0:T(8,128)(2,1)S(1)} %fusion.35), channel_id=1, source_target_pairs={{0,24},{8,0},{16,8},{24,16},{1,25},{9,1},{17,9},{25,17},{2,26},{10... | collective-permute-start | bytes 3145736 | tf_op jit(solution)/shard_map/ppermute | solution.py:17
  66.5 46.8 %collective-permute-start.1 = (bf16[16,2,128,128]{2,3,1,0:T(8,128)(2,1)S(1)}, bf16[16,2,128,128]{2,3,1,0:T(8,128)(2,1)S(1)}, u32[]{:S(2)}, u32[]{:S(2)}) collective-permute-start(bf16[16,2,128,128]{2,3,1,0:T(8,128)(2,1)S(1)} %fusion.35), channel_id=1, source_target_pairs={{0,16},{8,24},{16,0},{24,8},{1,17},{9,25},{17,1},{25,9},{2,18},{10... | collective-permute-start | bytes 3145736 | tf_op jit(solution)/shard_map/ppermute | solution.py:17
  123.6 1.4 copy-start.2
  123.6 4.7 %copy-start.1 = (f32[16,2,127,128]{2,3,1,0:T(8,128)}, f32[16,2,127,128]{2,3,1,0:T(8,128)S(1)}, u32[]{:S(2)}) copy-start(f32[16,2,127,128]{2,3,1,0:T(8,128)S(1)} %get-tuple-element.23) | copy-start | bytes 6242308
  124.3 4.0 %copy-start = (f32[16,2,1,128]{2,3,1,0:T(8,128)}, f32[16,2,1,128]{2,3,1,0:T(8,128)S(1)}, u32[]{:S(2)}) copy-start(f32[16,2,1,128]{2,3,1,0:T(8,128)S(1)} %get-tuple-element.26) | copy-start | bytes 49156
  147.6 4.0 %copy-start.3 = (f32[16,2,128,127]{2,3,1,0:T(8,128)S(1)}, f32[16,2,128,127]{2,3,1,0:T(8,128)}, u32[]{:S(2)}) copy-start(f32[16,2,128,127]{2,3,1,0:T(8,128)} %get-tuple-element.5) | copy-start | bytes 6242308
